TPU v7x, 32 devices: a whole 2x2x4 slice. The times are simulated.
32 devices in a mesh: rep: 16 (over z, y, x), tp: 2 (over core).
Axes of the slice: x: 2, y: 2, z: 4, core: 2. Of those that a mesh axis runs over, the one named last changes fastest.
Arguments:
- grads_narrow: bfloat16 [16, 1, 2, 1024, 512], P('rep', None, None, None, 'tp'), may hold values from -6 to 6
- errors_narrow: float32 [16, 1, 2, 1024, 512], P('rep', None, None, None, 'tp'), may hold values from -6 to 6
- starts_narrow: float32 [1, 2, 512, 32], P(None, None, 'tp'), may hold values from -6 to 6
- moment_narrow: float32 [1, 2, 524288], P(None, None, ('rep', 'tp')), may hold values from -0.75 to 0.75
- grads_square: bfloat16 [16, 1, 3, 1024, 1024], P('rep', None, None, None, 'tp'), may hold values from -6 to 6
- errors_square: float32 [16, 1, 3, 1024, 1024], P('rep', None, None, None, 'tp'), may hold values from -6 to 6
- starts_square: float32 [1, 3, 1024, 32], P(None, None, 'tp'), may hold values from -6 to 6
- moment_square: float32 [1, 3, 1048576], P(None, None, ('rep', 'tp')), may hold values from -0.75 to 0.75
Outputs:
- residue_narrow: float32 [16, 1, 2, 1024, 512], P('rep', None, None, None, 'tp')
- factor_narrow: float32 [1, 2, 512, 32], P(None, None, 'tp')
- velocity_narrow: float32 [1, 2, 524288], P(None, None, ('rep', 'tp'))
- residue_square: float32 [16, 1, 3, 1024, 1024], P('rep', None, None, None, 'tp')
- factor_square: float32 [1, 3, 1024, 32], P(None, None, 'tp')
- velocity_square: float32 [1, 3, 1048576], P(None, None, ('rep', 'tp'))
All inputs are finite; a program needn't handle non-finite values.
Results may differ from a plain program's by a relative error of at most 0.0003.
Values sent between devices are 32-bit elements; how exact they have to be, the bound alone decides.
A program may use at most 128 MiB of HBM per device.

v0:
```python
import jax
import jax.numpy as jnp
from jax import lax
from jax.sharding import PartitionSpec as P

ROUNDS = 2
NS_STEPS = 5


epsilon = 1e-06
momentum_decay = 0.9
highest = lax.Precision.HIGHEST


def orthonormal(panel):
    scaled = panel / (jnp.sqrt(jnp.sum(panel * panel)) + epsilon)
    for sweep in range(NS_STEPS):
        gram = lax.dot_general(scaled, scaled, (((0,), (0,)), ((), ())), precision=highest)
        scaled = 1.5 * scaled - 0.5 * jnp.dot(scaled, gram, precision=highest)
    return scaled


def left_product(matrix, factor):
    return jnp.dot(matrix, factor, precision=highest, preferred_element_type=jnp.float32)


def right_product(matrix, ortho):
    return lax.dot_general(matrix, ortho, (((0,), (0,)), ((), ())), precision=highest)


def outer_product(ortho, factor):
    return lax.dot_general(ortho, factor, (((1,), (1,)), ((), ())), precision=highest)


def on_device(
    grads_narrow,
    errors_narrow,
    starts_narrow,
    moment_narrow,
    grads_square,
    errors_square,
    starts_square,
    moment_square,
):
    replicas = lax.axis_size("rep")
    shards = lax.axis_size("tp")
    rep_index = lax.axis_index("rep")
    width = grads_narrow.shape[3]
    rows_dev = width // (replicas * shards)
    merged, factors, narrow_index, square_index = ([], [], [], [])
    for which in range(2):
        narrow_index.append(len(merged))
        merged.append(grads_narrow[0, 0, which].astype(jnp.float32) + errors_narrow[0, 0, which])
        factors.append(starts_narrow[0, which])
    for which in range(3):
        square_index.append(len(merged))
        merged.append(grads_square[0, 0, which].astype(jnp.float32) + errors_square[0, 0, which])
        factors.append(starts_square[0, which])
    total = len(merged)
    panels = [None] * total
    for turn in range(ROUNDS):
        partial_p = jnp.stack([left_product(merged[item], factors[item]) for item in range(total)])
        summed = lax.psum(partial_p, ("rep", "tp"))
        panels = [orthonormal(summed[item]) for item in range(total)]
        narrow_terms = jnp.stack(
            [right_product(merged[item], panels[item]) for item in narrow_index]
        )
        square_terms = jnp.stack(
            [right_product(merged[item], panels[item]) for item in square_index]
        )
        narrow_sum, square_sum = lax.psum((narrow_terms, square_terms), "rep")
        for place, item in enumerate(narrow_index):
            factors[item] = narrow_sum[place] / replicas
        for place, item in enumerate(square_index):
            factors[item] = square_sum[place] / replicas
    approx = [outer_product(panels[item], factors[item]) for item in range(total)]
    residues = [merged[item] - approx[item] for item in range(total)]
    first = rep_index * (shards * rows_dev)
    narrow_blocks = jnp.stack(
        [
            lax.dynamic_slice_in_dim(approx[item], first, shards * rows_dev, 0)
            for item in narrow_index
        ]
    )
    square_blocks = jnp.stack(
        [
            lax.dynamic_slice_in_dim(approx[item], first, shards * rows_dev, 0)
            for item in square_index
        ]
    )
    narrow_rows, square_rows = (
        lax.all_to_all(narrow_blocks, "tp", split_axis=1, concat_axis=2, tiled=True),
        lax.all_to_all(square_blocks, "tp", split_axis=1, concat_axis=2, tiled=True),
    )
    velocity_narrow = momentum_decay * moment_narrow + narrow_rows.reshape(moment_narrow.shape)
    velocity_square = momentum_decay * moment_square + square_rows.reshape(moment_square.shape)
    residue_narrow = jnp.stack([residues[item] for item in narrow_index]).reshape(
        grads_narrow.shape
    )
    residue_square = jnp.stack([residues[item] for item in square_index]).reshape(
        grads_square.shape
    )
    factor_narrow = jnp.stack([factors[item] for item in narrow_index]).reshape(starts_narrow.shape)
    factor_square = jnp.stack([factors[item] for item in square_index]).reshape(starts_square.shape)
    return (
        residue_narrow,
        factor_narrow,
        velocity_narrow,
        residue_square,
        factor_square,
        velocity_square,
    )


def solution(mesh):
    in_specs = (
        P("rep", None, None, None, "tp"),
        P("rep", None, None, None, "tp"),
        P(None, None, "tp", None),
        P(None, None, ("rep", "tp")),
        P("rep", None, None, None, "tp"),
        P("rep", None, None, None, "tp"),
        P(None, None, "tp", None),
        P(None, None, ("rep", "tp")),
    )
    out_specs = (
        P("rep", None, None, None, "tp"),
        P(None, None, "tp", None),
        P(None, None, ("rep", "tp")),
        P("rep", None, None, None, "tp"),
        P(None, None, "tp", None),
        P(None, None, ("rep", "tp")),
    )
    return jax.shard_map(
        on_device, mesh=mesh, in_specs=in_specs, out_specs=out_specs, check_vma=False
    )
```

profile of v0, /device:TPU:0, one launch (start us, length us, event | category | flops | bytes accessed | tf_op | source)
XLA Modules:
  0.0 653.4 jit_solution(221167027772143565)
XLA Ops:
  7.2 3.3 fusion.30
  10.5 3.2 fusion.29
  13.7 4.6 fusion.34
  18.3 4.1 fusion.46
  25.7 131.0 %all-reduce.7.cloned.1.call-done = f32[5,1024,32]{1,2,0:T(8,128)} async-done(((f32[5,1024,32]{1,2,0:T(8,128)}), f32[5,1024,32]{1,2,0:T(8,128)}) %all-reduce.7.cloned.1.call-update) | async-done | bytes 655376 | tf_op jit(solution)/shard_map/psum | solution.py:63
  164.1 3.0 fusion.117
  172.7 3.0 fusion.123
  181.3 3.0 fusion.129
  198.8 106.2 %all-reduce.13.cloned.1.call-done = (f32[2,256,32]{1,2,0:T(8,128)}, f32[3,512,32]{1,2,0:T(8,128)}) async-done(((f32[2,256,32]{1,2,0:T(8,128)}, f32[3,512,32]{1,2,0:T(8,128)}), (f32[2,256,32]{1,2,0:T(8,128)}, f32[3,512,32]{1,2,0:T(8,128)})) %all-reduce.13.cloned.1.call-update) | async-done | bytes 262160 | tf_op jit(solution)/shard_map/psum | solution.py:71
  305.0 3.3 fusion.28
  308.2 3.0 fusion.27
  311.3 4.4 fusion.40
  315.6 4.4 fusion.52
  320.0 4.4 fusion.64
  324.7 127.6 %all-reduce.9.cloned.1.call-done = f32[5,1024,32]{1,2,0:T(8,128)} async-done(((f32[5,1024,32]{1,2,0:T(8,128)}), f32[5,1024,32]{1,2,0:T(8,128)}) %all-reduce.9.cloned.1.call-update) | async-done | bytes 655376 | tf_op jit(solution)/shard_map/psum | solution.py:63
  459.7 3.7 fusion.120
  469.0 3.7 fusion.126
  478.2 3.7 fusion.132
  498.9 106.2 %all-reduce.11.cloned.1.call-done = (f32[2,256,32]{1,2,0:T(8,128)}, f32[3,512,32]{1,2,0:T(8,128)}) async-done(((f32[2,256,32]{1,2,0:T(8,128)}, f32[3,512,32]{1,2,0:T(8,128)}), (f32[2,256,32]{1,2,0:T(8,128)}, f32[3,512,32]{1,2,0:T(8,128)})) %all-reduce.11.cloned.1.call-update) | async-done | bytes 262160 | tf_op jit(solution)/shard_map/psum | solution.py:71
  614.5 6.1 fusion.26
  625.7 4.4 all_to_all.30
  632.8 4.0 all_to_all.31
  639.5 2.8 maximum_bitcast_fusion.1
  643.0 3.4 maximum_bitcast_fusion
  (227 shorter events, 84.4 us)
Async XLA Ops:
  7.2 6.5 %copy-start.32 = (f32[1,3,512,32]{2,3,1,0:T(8,128)S(1)}, f32[1,3,512,32]{2,3,1,0:T(8,128)}, u32[]{:S(2)}) copy-start(f32[1,3,512,32]{2,3,1,0:T(8,128)} %param.14) | copy-start | bytes 589828
  7.2 149.6 %all-reduce.7.cloned.1.call-start = ((), (), s32[]{:S(2)}) async-start(), calls=%async_computation.2 | async-start | bytes 1310720 | tf_op jit(solution)/shard_map/psum | solution.py:63
  7.2 11.1 %copy-start = (f32[1,1,3,1024,512]{4,3,2,1,0:T(8,128)S(1)}, f32[1,1,3,1024,512]{4,3,2,1,0:T(8,128)}, u32[]{:S(2)}) copy-start(f32[1,1,3,1024,512]{4,3,2,1,0:T(8,128)} %param.13) | copy-start | bytes 18874372
  25.1 279.8 %all-reduce.13.cloned.1.call-start = ((), (), s32[]{:S(2)}) async-start(), calls=%async_computation.5 | async-start | bytes 524288 | tf_op jit(solution)/shard_map/psum | solution.py:71
  198.7 253.6 %all-reduce.9.cloned.1.call-start = ((), (), s32[]{:S(2)}) async-start(), calls=%async_computation.3 | async-start | bytes 1310720 | tf_op jit(solution)/shard_map/psum | solution.py:63
  305.0 6.3 copy-start.33
  324.4 280.7 %all-reduce.11.cloned.1.call-start = ((), (), s32[]{:S(2)}) async-start(), calls=%async_computation.4 | async-start | bytes 524288 | tf_op jit(solution)/shard_map/psum | solution.py:71
  481.8 5.8 copy-start.5
  481.8 5.8 copy-start.10
  492.3 5.2 copy-start.34
  492.3 5.9 copy-start.26
  492.3 5.9 copy-start.27
  492.3 5.9 copy-start.28
  493.5 120.9 %slice-start = ((s8[6291456]{0:T(1024)(128)(4,1)}), s8[2097152]{0:T(1024)(128)(4,1)S(1)}, s32[]{:S(2)}) async-start(s8[6291456]{0:T(1024)(128)(4,1)} %bitcast.490), calls=%async_computation.6 | async-start | bytes 4194304
  605.1 9.3 %slice-start.1 = ((s8[6291456]{0:T(1024)(128)(4,1)}), s8[4194304]{0:T(1024)(128)(4,1)S(1)}, s32[]{:S(2)}) async-start(s8[6291456]{0:T(1024)(128)(4,1)} %bitcast.490), calls=%async_computation.7 | async-start | bytes 8388608
  614.4 6.1 copy-start.18
  614.5 6.1 copy-start.25
  614.5 7.1 %copy-start.20 = (f32[1024,32]{0,1:T(8,128)S(1)}, f32[1024,32]{0,1:T(8,128)}, u32[]{:S(2)}) copy-start(f32[1024,32]{0,1:T(8,128)} %copy-done.19) | copy-start | bytes 393220
  625.3 5.7 copy-start.24
  631.0 7.8 %copy-start.35 = (f32[1,256,32]{1,2,0:T(8,128)S(1)}, f32[1,256,32]{1,2,0:T(8,128)}, u32[]{:S(2)}) copy-start(f32[1,256,32]{1,2,0:T(8,128)} %get-tuple-element.40) | copy-start | bytes 98308
  631.0 7.8 %copy-start.36 = (f32[1,256,32]{1,2,0:T(8,128)S(1)}, f32[1,256,32]{1,2,0:T(8,128)}, u32[]{:S(2)}) copy-start(f32[1,256,32]{1,2,0:T(8,128)} %get-tuple-element.41) | copy-start | bytes 98308
  631.0 8.4 %copy-start.16 = (f32[1,1024,256]{2,1,0:T(8,128)S(1)}, f32[1,1024,256]{2,1,0:T(8,128)}, u32[]{:S(2)}) copy-start(f32[1,1024,256]{2,1,0:T(8,128)} %get-tuple-element.35) | copy-start | bytes 3145732
  632.6 9.7 %copy-start.31 = (f32[1,512,32]{1,2,0:T(8,128)S(1)}, f32[1,512,32]{1,2,0:T(8,128)}, u32[]{:S(2)}) copy-start(f32[1,512,32]{1,2,0:T(8,128)} %get-tuple-element.39) | copy-start | bytes 196612
  632.7 10.3 %copy-start.15 = (f32[1,1024,512]{2,1,0:T(8,128)S(1)}, f32[1,1024,512]{2,1,0:T(8,128)}, u32[]{:S(2)}) copy-start(f32[1,1024,512]{2,1,0:T(8,128)} %get-tuple-element.34) | copy-start | bytes 6291460
  (19 other events, 66.4 us)
Sparse Core Ops, SparseCore 0:
  25.3 131.4 all-reduce.6
  198.9 106.0 all-reduce.12
  324.5 127.7 all-reduce.8
  499.0 106.0 all-reduce.10
where the time goes:
time: 659 us; the launch traced here: 653 us
  waiting for transfers between devices  471 us (71%)
  matrix products  119 us (18%)
  other arithmetic  25.6 us (4%)
  between operations  22.7 us (3%)
  blocking collectives  8.4 us (1%)
    psum x2, waiting for transfers between devices, on_device(): summed = lax.psum(partial_p, ('rep', 'tp'))  259 us
    psum x2, waiting for transfers between devices, on_device(): narrow_sum, square_sum = lax.psum((narrow_terms, square_terms), 'rep')  212 us
    dot_general x10, matrix products, left_product(): jnp.dot(matrix, factor, precision=highest, preferred_element_type=jnp.flo...  37.3 us
    dot_general x50, matrix products, orthonormal(): scaled = 1.5 * scaled - 0.5 * jnp.dot(scaled, gram, precision=highest)  26 us
    dot_general x10, matrix products, right_product(): lax.dot_general(matrix, ortho, (((0,), (0,)), ((), ())), precision=highest)  24.8 us
    dot_general x50, matrix products, orthonormal(): lax.dot_general(scaled, scaled, (((0,), (0,)), ((), ())), precision=highest)  22.6 us
  transfers between devices with their start and end apart: 4, of which 4 were waited for; matrix products, arithmetic and copies ran while one was open for 0% of the time, Pallas kernels for 0%

commit v1 on v0

v1 whole, which is shorter than its diff:
```python
import functools

import jax
import jax.numpy as jnp
from jax import lax
from jax.experimental import pallas as pl
from jax.experimental.pallas import tpu as pltpu
from jax.sharding import PartitionSpec as P

ROUNDS = 2
NS_STEPS = 5
LANES = 128
BAND = 256
VMEM_LIMIT = 48 * 1024 * 1024

epsilon = 1e-06
momentum_decay = 0.9
highest = lax.Precision.HIGHEST
f32, bf16 = jnp.float32, jnp.bfloat16
MESH = pl.DeviceIdType.MESH


def split(x):
    hi = x.astype(bf16)
    lo = (x - hi.astype(f32)).astype(bf16)
    return hi, lo


def dot(a, b, dims, precision=None):
    return lax.dot_general(a, b, (dims, ((), ())), precision=precision, preferred_element_type=f32)


NN, NT, TN = ((1,), (0,)), ((1,), (1,)), ((0,), (0,))


def first_blocks(widths):
    first, at = [], 0
    for width in widths:
        first.append(at)
        at += width // LANES
    return first, at


def factor_of(ref, first, width, rank, offset=0):
    pieces = [
        ref[(offset + first + b) * rank : (offset + first + b + 1) * rank, :]
        for b in range(width // LANES)
    ]
    return jnp.concatenate(pieces, axis=1)


def left_band(out_ref, item, rank, stacked, hi, lo):
    both = dot(stacked, hi, NT)
    band = both[:rank] + both[rank:] + dot(stacked[:rank], lo, NT)
    for b in range(BAND // LANES):
        out_ref[b, item * rank : (item + 1) * rank, :] = band[:, b * LANES : (b + 1) * LANES]


def first_left_kernel(rank, gn, en, gs, es, sn, ss, panel, hn, ln, hs, ls, fn, fs):
    @pl.when(pl.program_id(0) == 0)
    def _():
        for start, keep in ((sn, fn), (ss, fs)):
            for which in range(start.shape[0]):
                keep[which] = jnp.concatenate(split(start[which].T), axis=0)

    item = 0
    for g, e, h, l, keep in ((gn, en, hn, ln, fn), (gs, es, hs, ls, fs)):
        for which in range(g.shape[0]):
            hi, lo = split(g[which].astype(f32) + e[which])
            h[which], l[which] = hi, lo
            left_band(panel, item, rank, keep[which], hi, lo)
            item += 1


def left_kernel(rank, replicas, factor, hn, ln, hs, ls, panel, fn, fs):
    counts = (hn.shape[0], hs.shape[0])
    widths = [hn.shape[2]] * counts[0] + [hs.shape[2]] * counts[1]
    first, _ = first_blocks(widths)

    @pl.when(pl.program_id(0) == 0)
    def _():
        item = 0
        for keep in (fn, fs):
            for which in range(keep.shape[0]):
                whole = factor_of(factor, first[item], widths[item], rank) / replicas
                keep[which] = jnp.concatenate(split(whole), axis=0)
                item += 1

    item = 0
    for h, l, keep in ((hn, ln, fn), (hs, ls, fs)):
        for which in range(h.shape[0]):
            left_band(panel, item, rank, keep[which], h[which], l[which])
            item += 1


def right_kernel(rank, items, panel, hn, ln, hs, ls, ortho, factor):
    step = pl.program_id(0)
    blocks = panel.shape[0]
    size = items * rank

    @pl.when(step == 0)
    def _():
        stacked = jnp.concatenate([panel[b] for b in range(blocks)], axis=1)
        scaled = []
        for item in range(items):
            part = stacked[item * rank : (item + 1) * rank]
            scaled.append(part / (jnp.sqrt(jnp.sum(part * part)) + epsilon))
        scaled = jnp.concatenate(scaled, axis=0)
        row = lax.broadcasted_iota(jnp.int32, (size, size), 0)
        column = lax.broadcasted_iota(jnp.int32, (size, size), 1)
        own = (row // rank) == (column // rank)
        identity = jnp.where(row == column, 1.0, 0.0).astype(f32)
        gram = jnp.where(own, dot(scaled, scaled, NT, highest), 0.0)
        total = None
        for sweep in range(NS_STEPS):
            turn = 1.5 * identity - 0.5 * gram
            total = turn if total is None else dot(turn, total, NN, highest)
            if sweep < NS_STEPS - 1:
                gram = dot(dot(turn, gram, NN, highest), turn, NN, highest)
        result = dot(total, scaled, NN, highest)
        for b in range(blocks):
            ortho[b] = result[:, b * LANES : (b + 1) * LANES]
        factor[...] = jnp.zeros_like(factor)

    per = BAND // LANES
    band = jnp.concatenate([ortho[step * per + b] for b in range(per)], axis=1)
    item = at = 0
    for h, l in ((hn, ln), (hs, ls)):
        for which in range(h.shape[0]):
            hi, lo = split(band[item * rank : (item + 1) * rank])
            both = dot(jnp.concatenate([hi, lo], axis=0), h[which], NN)
            term = both[:rank] + both[rank:] + dot(hi, l[which], NN)
            for b in range(h.shape[2] // LANES):
                factor[at : at + rank, :] += term[:, b * LANES : (b + 1) * LANES]
                at += rank
            item += 1


def last_kernel(
    rank, replicas, ortho, both, hn, ln, hs, ls, mn, ms,
    rn, rs, fn, fs, vn, vs, kn, ks, rows_n, rows_s,
):
    step = pl.program_id(0)
    counts = (hn.shape[0], hs.shape[0])
    widths = [hn.shape[2]] * counts[0] + [hs.shape[2]] * counts[1]
    first, blocks = first_blocks(widths)
    tp = lax.axis_index("tp")
    place = lax.axis_index("rep") * lax.axis_size("tp") + tp
    own = pl.multiple_of(tp * blocks * rank, blocks * rank)

    def wide(whole):
        hi, lo = split(whole)
        return jnp.concatenate([hi, hi, lo], axis=0)

    def tall(part):
        hi, lo = split(part)
        return jnp.concatenate([hi, lo, hi], axis=0)

    @pl.when(step == 0)
    def _():
        item = 0
        for f, k, m, v, rows_ref in ((fn, kn, mn, vn, rows_n), (fs, ks, ms, vs, rows_s)):
            rows = m.shape[1]
            at = place * rows
            block, inside = at // LANES, lax.rem(at, LANES)
            for which in range(f.shape[0]):
                width = widths[item]
                pieces = [
                    both[pl.ds(own + (first[item] + b) * rank, rank), :]
                    for b in range(width // LANES)
                ]
                mine = jnp.concatenate(pieces, axis=1) / replicas
                f[which] = mine.T
                k[which] = wide(mine)
                full = jnp.concatenate(
                    [factor_of(both, first[item], width, rank, core * blocks) for core in range(2)],
                    axis=1,
                )
                left = tall(ortho[block, item * rank : (item + 1) * rank, :])
                rows_ref[...] = dot(left, wide(full / replicas), TN)
                v[which] = momentum_decay * m[which] + rows_ref[
                    pl.ds(pl.multiple_of(inside, 8), rows), :
                ]
                item += 1

    per = BAND // LANES
    band = jnp.concatenate([ortho[step * per + b] for b in range(per)], axis=1)
    item = 0
    for h, l, k, r in ((hn, ln, kn, rn), (hs, ls, ks, rs)):
        for which in range(h.shape[0]):
            left = tall(band[item * rank : (item + 1) * rank])
            approx = dot(left, k[which], TN)
            r[which] = (h[which].astype(f32) + l[which].astype(f32)) - approx
            item += 1


NEAR = 4


def sum_kernel(replicas, over_tp, gather_tp, x, out, acc, in_tp, in_near, in_far, sems_s, sems_r):
    near = NEAR
    far = replicas // near
    rep, tp = lax.axis_index("rep"), lax.axis_index("tp")
    a, b = lax.rem(rep, near), rep // near
    other = {"tp": 1 - tp, "rep": rep}

    def near_id(j):
        return {"rep": b * near + lax.rem(a + j, near), "tp": tp}

    def far_id(j):
        return {"rep": lax.rem(b + j, far) * near + a, "tp": tp}

    barrier = pltpu.get_barrier_semaphore()
    partners = [near_id(j) for j in range(1, near)] + [far_id(j) for j in range(1, far)]
    if over_tp or gather_tp:
        partners.append(other)
    for partner in partners:
        pl.semaphore_signal(barrier, inc=1, device_id=partner, device_id_type=MESH)
    pl.semaphore_wait(barrier, len(partners))

    counter = [0]

    def send(src, dst, device):
        i = counter[0]
        counter[0] += 1
        copy = pltpu.make_async_remote_copy(
            src_ref=src, dst_ref=dst, send_sem=sems_s.at[i], recv_sem=sems_r.at[i],
            device_id=device, device_id_type=MESH,
        )
        copy.start()
        return copy

    def finish(copies):
        for copy in copies:
            copy.wait()

    def ds(at, size):
        return pl.ds(pl.multiple_of(at, 8), size)

    rows = x.shape[0]
    part = rows // 2 if over_tp else rows
    quarter = part // near
    slice_ = quarter // far

    if over_tp:
        base = tp * part
        finish([send(x.at[ds((1 - tp) * part, part)], in_tp, other)])
        acc[ds(base, part), :] = x[ds(base, part), :] + in_tp[...]
        src = acc
    else:
        base = tp * 0
        src = x

    finish([
        send(src.at[ds(base + lax.rem(a + j, near) * quarter, quarter)], in_near.at[j - 1], near_id(j))
        for j in range(1, near)
    ])
    mine = base + a * quarter
    value = src[ds(mine, quarter), :]
    for j in range(1, near):
        value = value + in_near[j - 1]
    acc[ds(mine, quarter), :] = value

    finish([
        send(acc.at[ds(mine + lax.rem(b + j, far) * slice_, slice_)], in_far.at[j - 1], far_id(j))
        for j in range(1, far)
    ])
    leaf = mine + b * slice_
    value = acc[ds(leaf, slice_), :]
    for j in range(1, far):
        value = value + in_far[j - 1]
    shift = tp * rows if gather_tp else 0
    out[ds(shift + leaf, slice_), :] = value

    def spread(at, size, ids):
        at = shift + at
        finish([send(out.at[ds(at, size)], out.at[ds(at, size)], device) for device in ids])

    spread(leaf, slice_, [far_id(j) for j in range(1, far)])
    spread(mine, quarter, [near_id(j) for j in range(1, near)])
    if over_tp:
        spread(base, part, [other])
    if gather_tp:
        spread(0, rows, [other])


def all_sum(x, replicas, over_tp, gather_tp, collective_id):
    rows = x.shape[0]
    far = replicas // NEAR
    part = rows // 2 if over_tp else rows
    quarter = part // NEAR
    copies = 2 * (NEAR - 1 + far - 1 + 1)
    return pl.pallas_call(
        functools.partial(sum_kernel, replicas, over_tp, gather_tp),
        out_shape=jax.ShapeDtypeStruct((rows * (2 if gather_tp else 1), LANES), f32),
        in_specs=[pl.BlockSpec(memory_space=pltpu.VMEM)],
        out_specs=pl.BlockSpec(memory_space=pltpu.VMEM),
        scratch_shapes=[
            pltpu.VMEM((rows, LANES), f32),
            pltpu.VMEM((part, LANES), f32),
            pltpu.VMEM((NEAR - 1, quarter, LANES), f32),
            pltpu.VMEM((far - 1, quarter // far, LANES), f32),
            pltpu.SemaphoreType.DMA((copies,)),
            pltpu.SemaphoreType.DMA((copies,)),
        ],
        compiler_params=pltpu.CompilerParams(
            collective_id=collective_id, has_side_effects=True, vmem_limit_bytes=VMEM_LIMIT
        ),
        name=f"all_sum_{collective_id}",
    )(x)


def padded_sum(x, replicas, over_tp, gather_tp, collective_id):
    rows = x.shape[0]
    unit = 8 * replicas * (2 if over_tp else 1)
    extra = -rows % unit
    if extra:
        x = jnp.pad(x, ((0, extra), (0, 0)))
    total = all_sum(x, replicas, over_tp, gather_tp, collective_id)
    if extra:
        if gather_tp:
            total = total.reshape(2, rows + extra, LANES)[:, :rows].reshape(2 * rows, LANES)
        else:
            total = total[:rows]
    return total


def on_device(gn, en, sn, mn, gs, es, ss, ms):
    replicas = lax.axis_size("rep")
    shape_gn, shape_gs, shape_sn, shape_ss = gn.shape, gs.shape, sn.shape, ss.shape
    shape_mn, shape_ms = mn.shape, ms.shape
    gn, en, gs, es = (
        x.reshape((x.shape[1] * x.shape[2],) + x.shape[3:]) for x in (gn, en, gs, es)
    )
    sn, ss = (x.reshape((-1,) + x.shape[2:]) for x in (sn, ss))
    cn, depth, wn = gn.shape
    cs, _, ws = gs.shape
    rank = sn.shape[-1]
    items = cn + cs
    steps, per, blocks = depth // BAND, BAND // LANES, depth // LANES
    factor_rows = (cn * wn + cs * ws) // LANES * rank
    mn = mn.reshape(cn, -1, 2 * wn)
    ms = ms.reshape(cs, -1, 2 * ws)

    band_n = pl.BlockSpec((cn, BAND, wn), lambda t: (0, t, 0))
    band_s = pl.BlockSpec((cs, BAND, ws), lambda t: (0, t, 0))
    bands = [band_n, band_n, band_s, band_s]

    def full(shape):
        return pl.BlockSpec(shape, lambda t: (0,) * len(shape))

    panel_band = pl.BlockSpec((per, items * rank, LANES), lambda t: (t, 0, 0))
    panel_shape = jax.ShapeDtypeStruct((blocks, items * rank, LANES), f32)
    keep = [pltpu.VMEM((cn, 2 * rank, wn), bf16), pltpu.VMEM((cs, 2 * rank, ws), bf16)]
    params = pltpu.CompilerParams(vmem_limit_bytes=VMEM_LIMIT)

    panel, hn, ln, hs, ls = pl.pallas_call(
        functools.partial(first_left_kernel, rank),
        grid=(steps,),
        in_specs=bands + [full(sn.shape), full(ss.shape)],
        out_specs=[panel_band] + bands,
        out_shape=[
            panel_shape,
            jax.ShapeDtypeStruct(gn.shape, bf16),
            jax.ShapeDtypeStruct(gn.shape, bf16),
            jax.ShapeDtypeStruct(gs.shape, bf16),
            jax.ShapeDtypeStruct(gs.shape, bf16),
        ],
        scratch_shapes=keep,
        compiler_params=params,
        name="first_left",
    )(gn, en, gs, es, sn, ss)

    for turn in range(ROUNDS):
        if turn:
            panel = pl.pallas_call(
                functools.partial(left_kernel, rank, replicas),
                grid=(steps,),
                in_specs=[full(factor.shape)] + bands,
                out_specs=panel_band,
                out_shape=panel_shape,
                scratch_shapes=keep,
                compiler_params=params,
                name="left",
            )(factor, hn, ln, hs, ls)
        panel = padded_sum(panel.reshape(-1, LANES), replicas, True, False, 0)
        panel = panel.reshape(panel_shape.shape)
        ortho, factor = pl.pallas_call(
            functools.partial(right_kernel, rank, items),
            grid=(steps,),
            in_specs=[full(panel_shape.shape)] + bands,
            out_specs=[full(panel_shape.shape), full((factor_rows, LANES))],
            out_shape=[panel_shape, jax.ShapeDtypeStruct((factor_rows, LANES), f32)],
            compiler_params=params,
            name="right",
        )(panel, hn, ln, hs, ls)
        final = turn == ROUNDS - 1
        factor = padded_sum(factor, replicas, False, final, 2 if final else 1)

    rn, rs, fn, fs, vn, vs = pl.pallas_call(
        functools.partial(last_kernel, rank, replicas),
        grid=(steps,),
        in_specs=[full(panel_shape.shape), full(factor.shape)]
        + bands
        + [full(mn.shape), full(ms.shape)],
        out_specs=[
            band_n, band_s, full(sn.shape), full(ss.shape), full(mn.shape), full(ms.shape),
        ],
        out_shape=[
            jax.ShapeDtypeStruct(x.shape, f32) for x in (gn, gs, sn, ss, mn, ms)
        ],
        scratch_shapes=[
            pltpu.VMEM((cn, 3 * rank, wn), bf16),
            pltpu.VMEM((cs, 3 * rank, ws), bf16),
            pltpu.VMEM((LANES, 2 * wn), f32),
            pltpu.VMEM((LANES, 2 * ws), f32),
        ],
        compiler_params=params,
        name="last",
    )(ortho, factor, hn, ln, hs, ls, mn, ms)
    return (
        rn.reshape(shape_gn),
        fn.reshape(shape_sn),
        vn.reshape(shape_mn),
        rs.reshape(shape_gs),
        fs.reshape(shape_ss),
        vs.reshape(shape_ms),
    )


def solution(mesh):
    in_specs = (
        P("rep", None, None, None, "tp"),
        P("rep", None, None, None, "tp"),
        P(None, None, "tp", None),
        P(None, None, ("rep", "tp")),
        P("rep", None, None, None, "tp"),
        P("rep", None, None, None, "tp"),
        P(None, None, "tp", None),
        P(None, None, ("rep", "tp")),
    )
    out_specs = (
        P("rep", None, None, None, "tp"),
        P(None, None, "tp", None),
        P(None, None, ("rep", "tp")),
        P("rep", None, None, None, "tp"),
        P(None, None, "tp", None),
        P(None, None, ("rep", "tp")),
    )
    return jax.shard_map(
        on_device, mesh=mesh, in_specs=in_specs, out_specs=out_specs, check_vma=False
    )
```

time: 659 us -> 141 us (0.21)
  waiting for transfers between devices: 471 us -> 0 us
  Pallas kernels: 0 us -> 131 us
  matrix products: 119 us -> 0 us
  other arithmetic: 25.6 us -> 2.07 us
  between operations: 22.7 us -> 0.73 us
  blocking collectives: 8.4 us -> 0 us
    psum x4 -> x0, waiting for transfers between devices: 471 us -> none  [the longest x2 259 us: on_device(): summed = lax.psum(partial_p, ('rep', 'tp'))]
    pallas_call x0 -> x9, Pallas kernels: none -> 131 us  [the longest x4 88.9 us: all_sum(): pl.pallas_call(functools.partial(sum_kernel, replicas, over_tp, gather_tp...]
    dot_general x125 -> x0, matrix products: 119 us -> none  [the longest x10 37.3 us: left_product(): jnp.dot(matrix, factor, precision=highest, preferred_element_type=jnp.flo...]
    another operation x8 -> x0, other arithmetic: 10.9 us -> none  [the longest x1 6.05 us: on_device(): jnp.stack([residues[item] for item in square_index])]
    all_to_all x2 -> x0, blocking collectives: 8.4 us -> none  [the longest x1 4.43 us: on_device(): lax.all_to_all(square_blocks, 'tp', split_axis=1, concat_axis=2, tiled=True)]
    reshape x4 -> x0, other arithmetic: 7.57 us -> none  [the longest x1 3.41 us: on_device(): jnp.stack([residues[item] for item in square_index])]
  transfers between devices with their start and end apart: 4 -> 0, of which waited for: 4 -> 0; matrix products, arithmetic and copies ran while one was open for 0% -> 0% of each run, Pallas kernels for 0% -> 0%
where the time goes in v1:
time: 141 us
  Pallas kernels  131 us (93%)
  local copies, waits for them, and re-layouts  7.04 us (5%)
  other arithmetic  2.07 us (1%)
    pallas_call x4, Pallas kernels, all_sum(): pl.pallas_call(functools.partial(sum_kernel, replicas, over_tp, gather_tp...  88.9 us
    pallas_call x2, Pallas kernels, on_device(): pl.pallas_call(functools.partial(right_kernel, rank, items), grid=(steps,...  20.6 us
    pallas_call x1, Pallas kernels, on_device(): pl.pallas_call(functools.partial(first_left_kernel, rank), grid=(steps,),...  8.85 us
    pallas_call x1, Pallas kernels, on_device(): pl.pallas_call(functools.partial(last_kernel, rank, replicas), grid=(step...  7.64 us
    unnamed x10, local copies, waits for them, and re-layouts  5.07 us
    pallas_call x1, Pallas kernels, on_device(): pl.pallas_call(functools.partial(left_kernel, rank, replicas), grid=(step...  4.83 us

profile of v1, /device:TPU:0, one launch (start us, length us, event | category | flops | bytes accessed | tf_op | source)
XLA Modules:
  0.0 140.7 jit_solution(18066393768926149852)
XLA Ops:
  0.6 0.0 copy-start.1
  0.6 1.0 copy.29
  1.7 1.0 copy.19
  2.6 2.1 %reduce = f32[3,32768]{1,0:T(4,128)S(1)} reduce(f32[1,3,32768]{2,0,1:T(1,128)} %param.15, f32[]{:T(128)} %constant.4), dimensions={0}, to_apply=%param.15.reduce_sub_computation | reduce | bytes 786436 | tf_op args[7]
  4.7 0.2 copy.28
  4.9 1.2 copy.20
  6.1 0.0 copy-done.1
  6.2 8.8 %first_left.1 = (f32[8,160,128]{2,1,0:T(8,128)S(1)}, bf16[2,1024,256]{2,1,0:T(8,128)(2,1)S(1)}, bf16[2,1024,256]{2,1,0:T(8,128)(2,1)S(1)}, bf16[3,1024,512]{2,1,0:T(8,128)(2,1)}, bf16[3,1024,512]{2,1,0:T(8,128)(2,1)}) custom-call(bf16[2,1024,256]{2,1,0:T(8,128)(2,1)S(1)} %bitcast.28, f32[2,1024,256]{2,1,0:T(8,128)} %bitcast.37, ...), custom_call_target="tpu_custom_call" | custom-call | tf_op jit(solution)/shard_map/first_left/pallas_call | solution.py:357
  15.0 26.7 %all_sum_0.2 = f32[1280,128]{1,0:T(8,128)S(1)} custom-call(f32[1280,128]{1,0:T(8,128)S(1)} %bitcast.31), custom_call_target="tpu_custom_call" | custom-call | tf_op jit(solution)/shard_map/all_sum_0/pallas_call | solution.py:293
  41.7 0.0 copy-start
  41.7 10.7 %right.2 = (f32[8,160,128]{2,1,0:T(8,128)}, f32[512,128]{1,0:T(8,128)S(1)}) custom-call(f32[8,160,128]{2,1,0:T(8,128)S(1)} %bitcast.24, bf16[2,1024,256]{2,1,0:T(8,128)(2,1)S(1)} %get-tuple-element.21.hn, bf16[2,1024,256]{2,1,0:T(8,128)(2,1)S(1)} %get-tuple-element.22.ln, bf16[3,1024,512]{2,1,0:T(8,128)(2,1)} %get-tuple-element.23.hs, ...), custom_call_target="tpu_custom_call" | custom-call | tf_op jit(solution)/shard_map/right/pallas_call | solution.py:388
  52.4 19.0 %all_sum_1.1.factor = f32[512,128]{1,0:T(8,128)S(1)} custom-call(f32[512,128]{1,0:T(8,128)S(1)} %get-tuple-element.25.x), custom_call_target="tpu_custom_call" | custom-call | tf_op jit(solution)/shard_map/all_sum_1/pallas_call | solution.py:293
  71.4 0.0 copy-done
  71.4 4.8 %left.1 = f32[8,160,128]{2,1,0:T(8,128)S(1)} custom-call(f32[512,128]{1,0:T(8,128)S(1)} %all_sum_1.1.factor, bf16[2,1024,256]{2,1,0:T(8,128)(2,1)S(1)} %get-tuple-element.21.hn, bf16[2,1024,256]{2,1,0:T(8,128)(2,1)S(1)} %get-tuple-element.22.ln, bf16[3,1024,512]{2,1,0:T(8,128)(2,1)S(1)} %copy-done, bf16[3,1024,512]{2,1,0:T(8,128)(2,1)} %get-tuple-element.24.ls), custom_call_target="tpu_custom_call" | custom-call | tf_op jit(solution)/shard_map/left/pallas_call | solution.py:376
  76.3 23.1 %all_sum_0.3 = f32[1280,128]{1,0:T(8,128)S(1)} custom-call(f32[1280,128]{1,0:T(8,128)S(1)} %bitcast.26), custom_call_target="tpu_custom_call" | custom-call | tf_op jit(solution)/shard_map/all_sum_0/pallas_call | solution.py:293
  99.4 9.9 %right.3 = (f32[8,160,128]{2,1,0:T(8,128)S(1)}, f32[512,128]{1,0:T(8,128)S(1)}) custom-call(f32[8,160,128]{2,1,0:T(8,128)S(1)} %bitcast.25, bf16[2,1024,256]{2,1,0:T(8,128)(2,1)S(1)} %get-tuple-element.21.hn, bf16[2,1024,256]{2,1,0:T(8,128)(2,1)S(1)} %get-tuple-element.22.ln, bf16[3,1024,512]{2,1,0:T(8,128)(2,1)} %get-tuple-element.23.hs, ...), custom_call_target="tpu_custom_call" | custom-call | tf_op jit(solution)/shard_map/right/pallas_call | solution.py:388
  109.3 20.2 %all_sum_2.1.both = f32[1024,128]{1,0:T(8,128)S(1)} custom-call(f32[512,128]{1,0:T(8,128)S(1)} %get-tuple-element.27.x), custom_call_target="tpu_custom_call" | custom-call | tf_op jit(solution)/shard_map/all_sum_2/pallas_call | solution.py:293
  129.5 7.6 %last.1 = (f32[2,1024,256]{2,1,0:T(8,128)}, f32[3,1024,512]{2,1,0:T(8,128)}, f32[2,256,32]{2,1,0:T(8,128)S(1)}, f32[3,512,32]{2,1,0:T(8,128)S(1)}, f32[2,32,512]...) custom-call(f32[8,160,128]{2,1,0:T(8,128)S(1)} %get-tuple-element.26.ortho, f32[1024,128]{1,0:T(8,128)S(1)} %all_sum_2.1.both, ...), custom_call_target="tpu_custom_call" | custom-call | tf_op jit(solution)/shard_map/last/pallas_call | solution.py:400
  137.1 0.7 copy.21
  137.8 0.8 reshape.80
  138.6 0.9 copy.22
  139.5 1.2 reshape.84
Async XLA Ops:
  0.6 5.5 %copy-start.1 = (bf16[1,1,2,1024,256]{4,3,2,1,0:T(8,128)(2,1)S(1)}, bf16[1,1,2,1024,256]{4,3,2,1,0:T(8,128)(2,1)}, u32[]{:S(2)}) copy-start(bf16[1,1,2,1024,256]{4,3,2,1,0:T(8,128)(2,1)} %param.8) | copy-start | bytes 3145732
  41.7 29.7 %copy-start = (bf16[3,1024,512]{2,1,0:T(8,128)(2,1)S(1)}, bf16[3,1024,512]{2,1,0:T(8,128)(2,1)}, u32[]{:S(2)}) copy-start(bf16[3,1024,512]{2,1,0:T(8,128)(2,1)} %get-tuple-element.23.hs) | copy-start | bytes 9437188

commit v2 on v1

--- a/solution.py
+++ b/solution.py
@@ -11,7 +11,7 @@
 NS_STEPS = 5
 LANES = 128
 BAND = 256
-VMEM_LIMIT = 48 * 1024 * 1024
+VMEM_LIMIT = 24 * 1024 * 1024
 
 epsilon = 1e-06
 momentum_decay = 0.9
@@ -61,7 +61,7 @@
     def _():
         for start, keep in ((sn, fn), (ss, fs)):
             for which in range(start.shape[0]):
-                keep[which] = jnp.concatenate(split(start[which].T), axis=0)
+                keep[which] = jnp.concatenate(split(start[which]), axis=0)
 
     item = 0
     for g, e, h, l, keep in ((gn, en, hn, ln, fn), (gs, es, hs, ls, fs)):
@@ -160,7 +160,9 @@
     def _():
         item = 0
         for f, k, m, v, rows_ref in ((fn, kn, mn, vn, rows_n), (fs, ks, ms, vs, rows_s)):
-            rows = m.shape[1]
+            per_row = rows_ref.shape[0]
+            rows = m.shape[0] // (f.shape[0] * per_row)
+            interleaved = f is fn
             at = place * rows
             block, inside = at // LANES, lax.rem(at, LANES)
             for which in range(f.shape[0]):
@@ -170,17 +172,25 @@
                     for b in range(width // LANES)
                 ]
                 mine = jnp.concatenate(pieces, axis=1) / replicas
-                f[which] = mine.T
+                f[which] = mine
                 k[which] = wide(mine)
                 full = jnp.concatenate(
                     [factor_of(both, first[item], width, rank, core * blocks) for core in range(2)],
                     axis=1,
                 )
                 left = tall(ortho[block, item * rank : (item + 1) * rank, :])
-                rows_ref[...] = dot(left, wide(full / replicas), TN)
-                v[which] = momentum_decay * m[which] + rows_ref[
-                    pl.ds(pl.multiple_of(inside, 8), rows), :
-                ]
+                approx = dot(left, wide(full / replicas), TN)
+                for c in range(per_row):
+                    rows_ref[c] = approx[:, c * LANES : (c + 1) * LANES]
+                for c in range(per_row):
+                    if interleaved:
+                        spot = pl.ds(c * f.shape[0] + which, rows, stride=per_row * f.shape[0])
+                    else:
+                        spot = pl.ds(which * rows * per_row + c, rows, stride=per_row)
+                    v[spot, :] = (
+                        momentum_decay * m[spot, :]
+                        + rows_ref[c, pl.ds(pl.multiple_of(inside, 8), rows), :]
+                    )
                 item += 1
 
     per = BAND // LANES
@@ -197,7 +207,18 @@
 NEAR = 4
 
 
-def sum_kernel(replicas, over_tp, gather_tp, x, out, acc, in_tp, in_near, in_far, sems_s, sems_r):
+def chunks_of(part, replicas):
+    unit = 8 * replicas
+    units = part // unit
+    lead = units - (2 * units) // 5
+    pieces = [(0, lead * unit, True)]
+    if units > lead:
+        pieces.append((lead * unit, part - lead * unit, False))
+    return pieces
+
+
+def sum_kernel(replicas, over_tp, gather_tp, pieces, x, out, acc, in_tp, *rest):
+    landing, (sems_s, sems_r) = rest[:-2], rest[-2:]
     near = NEAR
     far = replicas // near
     rep, tp = lax.axis_index("rep"), lax.axis_index("tp")
@@ -239,70 +260,95 @@
 
     rows = x.shape[0]
     part = rows // 2 if over_tp else rows
-    quarter = part // near
-    slice_ = quarter // far
+    base = tp * part if over_tp else 0
+    shift = tp * rows if gather_tp else 0
+    src = acc if over_tp else x
+    levels = [(near, a, near_id), (far, b, far_id)]
+    order = [levels if near_first else levels[::-1] for _, _, near_first in pieces]
+    count = len(pieces)
+    pending = [[] for _ in pieces]
+
+    def scatter(k, ref, at, size, level):
+        groups, me, ids = order[k][level]
+        share = size // groups
+        pending[k] = [
+            send(
+                ref.at[ds(at + lax.rem(me + j, groups) * share, share)],
+                landing[2 * k + level].at[j - 1],
+                ids(j),
+            )
+            for j in range(1, groups)
+        ]
+
+    def gather(k, at, size, devices):
+        view = out.at[ds(shift + at, size)]
+        pending[k] = [send(view, view, device) for device in devices]
+
+    def reduced(k, ref, at, size, level):
+        groups, me, _ = order[k][level]
+        share = size // groups
+        mine = at + me * share
+        value = ref[ds(mine, share), :]
+        for j in range(1, groups):
+            value = value + landing[2 * k + level][j - 1]
+        return mine, share, value
 
     if over_tp:
-        base = tp * part
-        finish([send(x.at[ds((1 - tp) * part, part)], in_tp, other)])
-        acc[ds(base, part), :] = x[ds(base, part), :] + in_tp[...]
-        src = acc
-    else:
-        base = tp * 0
-        src = x
-
-    finish([
-        send(src.at[ds(base + lax.rem(a + j, near) * quarter, quarter)], in_near.at[j - 1], near_id(j))
-        for j in range(1, near)
-    ])
-    mine = base + a * quarter
-    value = src[ds(mine, quarter), :]
-    for j in range(1, near):
-        value = value + in_near[j - 1]
-    acc[ds(mine, quarter), :] = value
-
-    finish([
-        send(acc.at[ds(mine + lax.rem(b + j, far) * slice_, slice_)], in_far.at[j - 1], far_id(j))
-        for j in range(1, far)
-    ])
-    leaf = mine + b * slice_
-    value = acc[ds(leaf, slice_), :]
-    for j in range(1, far):
-        value = value + in_far[j - 1]
-    shift = tp * rows if gather_tp else 0
-    out[ds(shift + leaf, slice_), :] = value
-
-    def spread(at, size, ids):
-        at = shift + at
-        finish([send(out.at[ds(at, size)], out.at[ds(at, size)], device) for device in ids])
-
-    spread(leaf, slice_, [far_id(j) for j in range(1, far)])
-    spread(mine, quarter, [near_id(j) for j in range(1, near)])
-    if over_tp:
-        spread(base, part, [other])
-    if gather_tp:
-        spread(0, rows, [other])
+        for k, (start, size, _) in enumerate(pieces):
+            theirs = x.at[ds((1 - tp) * part + start, size)]
+            pending[k] = [send(theirs, in_tp.at[pl.ds(start, size)], other)]
+    for k, (start, size, _) in enumerate(pieces):
+        if over_tp:
+            finish(pending[k])
+            acc[ds(base + start, size), :] = (
+                x[ds(base + start, size), :] + in_tp[pl.ds(start, size), :]
+            )
+        scatter(k, src, base + start, size, 0)
+    held = []
+    for k, (start, size, _) in enumerate(pieces):
+        finish(pending[k])
+        mine, share, value = reduced(k, src, base + start, size, 0)
+        acc[ds(mine, share), :] = value
+        held.append((mine, share))
+        scatter(k, acc, mine, share, 1)
+    for k in range(count):
+        finish(pending[k])
+        leaf, share, value = reduced(k, acc, held[k][0], held[k][1], 1)
+        out[ds(shift + leaf, share), :] = value
+        groups, _, ids = order[k][1]
+        gather(k, leaf, share, [ids(j) for j in range(1, groups)])
+    for k in range(count):
+        finish(pending[k])
+        groups, _, ids = order[k][0]
+        gather(k, held[k][0], held[k][1], [ids(j) for j in range(1, groups)])
+    for k, (start, size, _) in enumerate(pieces):
+        finish(pending[k])
+        pending[k] = []
+        if over_tp or gather_tp:
+            gather(k, base + start, size, [other])
+    for k in range(count):
+        finish(pending[k])
 
 
 def all_sum(x, replicas, over_tp, gather_tp, collective_id):
     rows = x.shape[0]
     far = replicas // NEAR
     part = rows // 2 if over_tp else rows
-    quarter = part // NEAR
-    copies = 2 * (NEAR - 1 + far - 1 + 1)
+    pieces = chunks_of(part, replicas)
+    copies = 2 * (NEAR - 1 + far - 1 + 1) * len(pieces)
+    landing = []
+    for _, size, near_first in pieces:
+        for groups in (NEAR, far) if near_first else (far, NEAR):
+            size = size // groups
+            landing.append(pltpu.VMEM((groups - 1, size, LANES), f32))
     return pl.pallas_call(
-        functools.partial(sum_kernel, replicas, over_tp, gather_tp),
+        functools.partial(sum_kernel, replicas, over_tp, gather_tp, pieces),
         out_shape=jax.ShapeDtypeStruct((rows * (2 if gather_tp else 1), LANES), f32),
         in_specs=[pl.BlockSpec(memory_space=pltpu.VMEM)],
         out_specs=pl.BlockSpec(memory_space=pltpu.VMEM),
-        scratch_shapes=[
-            pltpu.VMEM((rows, LANES), f32),
-            pltpu.VMEM((part, LANES), f32),
-            pltpu.VMEM((NEAR - 1, quarter, LANES), f32),
-            pltpu.VMEM((far - 1, quarter // far, LANES), f32),
-            pltpu.SemaphoreType.DMA((copies,)),
-            pltpu.SemaphoreType.DMA((copies,)),
-        ],
+        scratch_shapes=[pltpu.VMEM((rows, LANES), f32), pltpu.VMEM((part, LANES), f32)]
+        + landing
+        + [pltpu.SemaphoreType.DMA((copies,)), pltpu.SemaphoreType.DMA((copies,))],
         compiler_params=pltpu.CompilerParams(
             collective_id=collective_id, has_side_effects=True, vmem_limit_bytes=VMEM_LIMIT
         ),
@@ -332,15 +378,15 @@
     gn, en, gs, es = (
         x.reshape((x.shape[1] * x.shape[2],) + x.shape[3:]) for x in (gn, en, gs, es)
     )
-    sn, ss = (x.reshape((-1,) + x.shape[2:]) for x in (sn, ss))
+    sn, ss = (jnp.swapaxes(x.reshape((-1,) + x.shape[2:]), 1, 2) for x in (sn, ss))
     cn, depth, wn = gn.shape
     cs, _, ws = gs.shape
-    rank = sn.shape[-1]
+    rank = sn.shape[1]
     items = cn + cs
     steps, per, blocks = depth // BAND, BAND // LANES, depth // LANES
     factor_rows = (cn * wn + cs * ws) // LANES * rank
-    mn = mn.reshape(cn, -1, 2 * wn)
-    ms = ms.reshape(cs, -1, 2 * ws)
+    mn = jnp.swapaxes(mn.reshape(cn, -1, LANES), 0, 1).reshape(-1, LANES)
+    ms = ms.reshape(-1, LANES)
 
     band_n = pl.BlockSpec((cn, BAND, wn), lambda t: (0, t, 0))
     band_s = pl.BlockSpec((cs, BAND, ws), lambda t: (0, t, 0))
@@ -412,18 +458,18 @@
         scratch_shapes=[
             pltpu.VMEM((cn, 3 * rank, wn), bf16),
             pltpu.VMEM((cs, 3 * rank, ws), bf16),
-            pltpu.VMEM((LANES, 2 * wn), f32),
-            pltpu.VMEM((LANES, 2 * ws), f32),
+            pltpu.VMEM((2 * wn // LANES, LANES, LANES), f32),
+            pltpu.VMEM((2 * ws // LANES, LANES, LANES), f32),
         ],
         compiler_params=params,
         name="last",
     )(ortho, factor, hn, ln, hs, ls, mn, ms)
     return (
         rn.reshape(shape_gn),
-        fn.reshape(shape_sn),
-        vn.reshape(shape_mn),
+        jnp.swapaxes(fn, 1, 2).reshape(shape_sn),
+        jnp.swapaxes(vn.reshape(-1, cn, LANES), 0, 1).reshape(shape_mn),
         rs.reshape(shape_gs),
-        fs.reshape(shape_ss),
+        jnp.swapaxes(fs, 1, 2).reshape(shape_ss),
         vs.reshape(shape_ms),
     )
 

time: 141 us -> 124 us (0.88)
  Pallas kernels: 131 us -> 114 us
  local copies, waits for them, and re-layouts: 7.04 us -> 9.26 us
  other arithmetic: 2.07 us -> 0 us
    pallas_call x4, Pallas kernels: 88.9 us -> 84 us  [all_sum(): pl.pallas_call(functools.partial(sum_kernel, replicas, over_tp, gather_tp...]
    pallas_call x2, Pallas kernels: 20.6 us -> 16.3 us  [on_device(): pl.pallas_call(functools.partial(right_kernel, rank, items), grid=(steps,...]
    pallas_call x1, Pallas kernels: 8.85 us -> 4.65 us  [on_device(): pl.pallas_call(functools.partial(first_left_kernel, rank), grid=(steps,),...]
    unnamed x10 -> x16, local copies, waits for them, and re-layouts: 5.07 us -> 9.26 us
    pallas_call x1, Pallas kernels: 7.64 us -> 5.44 us  [on_device(): pl.pallas_call(functools.partial(last_kernel, rank, replicas), grid=(step...]
    unnamed x1 -> x0, other arithmetic: 2.07 us -> none
    reshape x2 -> x0, local copies, waits for them, and re-layouts: 1.97 us -> none  [the longest x1 1.21 us: on_device(): vs.reshape(shape_ms)]
where the time goes in v2:
time: 124 us
  Pallas kernels  114 us (92%)
  local copies, waits for them, and re-layouts  9.26 us (7%)
    pallas_call x4, Pallas kernels, all_sum(): pl.pallas_call(functools.partial(sum_kernel, replicas, over_tp, gather_tp...  84 us
    pallas_call x2, Pallas kernels, on_device(): pl.pallas_call(functools.partial(right_kernel, rank, items), grid=(steps,...  16.3 us
    unnamed x16, local copies, waits for them, and re-layouts  9.26 us
    pallas_call x1, Pallas kernels, on_device(): pl.pallas_call(functools.partial(last_kernel, rank, replicas), grid=(step...  5.44 us
    pallas_call x1, Pallas kernels, on_device(): pl.pallas_call(functools.partial(first_left_kernel, rank), grid=(steps,),...  4.65 us
    pallas_call x1, Pallas kernels, on_device(): pl.pallas_call(functools.partial(left_kernel, rank, replicas), grid=(step...  3.54 us

profile of v2, /device:TPU:0, one launch (start us, length us, event | category | flops | bytes accessed | tf_op | source)
XLA Modules:
  0.0 124.0 jit_solution(12247808530668392650)
XLA Ops:
  0.6 0.0 copy-start
  0.6 2.8 %copy-done = f32[1,1,3,1024,512]{4,3,2,1,0:T(8,128)S(1)} copy-done((f32[1,1,3,1024,512]{4,3,2,1,0:T(8,128)S(1)}, f32[1,1,3,1024,512]{4,3,2,1,0:T(8,128)}, u32[]{:S(2)}) %copy-start) | copy-done | bytes 6291480
  3.4 0.0 copy-start.1
  3.4 1.9 %copy-done.1 = bf16[1,1,3,1024,512]{4,3,2,1,0:T(8,128)(2,1)S(1)} copy-done((bf16[1,1,3,1024,512]{4,3,2,1,0:T(8,128)(2,1)S(1)}, bf16[1,1,3,1024,512]{4,3,2,1,0:T(8,128)(2,1)}, u32[]{:S(2)}) %copy-start.1) | copy-done | bytes 3145752
  5.3 0.0 copy-start.2
  5.3 1.6 %copy-done.2 = f32[1,1,2,1024,256]{4,3,2,1,0:T(8,128)S(1)} copy-done((f32[1,1,2,1024,256]{4,3,2,1,0:T(8,128)S(1)}, f32[1,1,2,1024,256]{4,3,2,1,0:T(8,128)}, u32[]{:S(2)}) %copy-start.2) | copy-done | bytes 2097176
  6.9 0.0 copy-start.3
  6.9 1.2 copy-done.3
  8.1 0.0 copy-start.5
  8.1 0.9 copy-done.5
  9.1 0.8 copy-done.7
  9.9 4.6 %first_left.1 = (f32[8,160,128]{2,1,0:T(8,128)S(1)}, bf16[2,1024,256]{2,1,0:T(8,128)(2,1)S(1)}, bf16[2,1024,256]{2,1,0:T(8,128)(2,1)S(1)}, bf16[3,1024,512]{2,1,0:T(8,128)(2,1)S(1)}, bf16[3,1024,512]{2,1,0:T(8,128)(2,1)S(1)}) custom-call(bf16[2,1024,256]{2,1,0:T(8,128)(2,1)S(1)} %bitcast.40, f32[2,1024,256]{2,1,0:T(8,128)S(1)} %bitcast.39, ...), custom_call_target="tpu_custom_call" | custom-call | tf_op jit(solution)/shard_map/first_left/pallas_call | solution.py:403
  14.5 24.5 %all_sum_0.2 = f32[1280,128]{1,0:T(8,128)S(1)} custom-call(f32[1280,128]{1,0:T(8,128)S(1)} %bitcast.41), custom_call_target="tpu_custom_call" | custom-call | tf_op jit(solution)/shard_map/all_sum_0/pallas_call | solution.py:344
  39.1 8.4 %right.2 = (f32[8,160,128]{2,1,0:T(8,128)}, f32[512,128]{1,0:T(8,128)S(1)}) custom-call(f32[8,160,128]{2,1,0:T(8,128)S(1)} %bitcast.36, bf16[2,1024,256]{2,1,0:T(8,128)(2,1)S(1)} %get-tuple-element.21.hn, bf16[2,1024,256]{2,1,0:T(8,128)(2,1)S(1)} %get-tuple-element.22.ln, bf16[3,1024,512]{2,1,0:T(8,128)(2,1)S(1)} %get-tuple-element.23.hs, ...), custom_call_target="tpu_custom_call" | custom-call | tf_op jit(solution)/shard_map/right/pallas_call | solution.py:434
  47.5 18.8 %all_sum_1.1.factor = f32[512,128]{1,0:T(8,128)S(1)} custom-call(f32[512,128]{1,0:T(8,128)S(1)} %get-tuple-element.25.x), custom_call_target="tpu_custom_call" | custom-call | tf_op jit(solution)/shard_map/all_sum_1/pallas_call | solution.py:344
  66.3 3.5 %left.1 = f32[8,160,128]{2,1,0:T(8,128)S(1)} custom-call(f32[512,128]{1,0:T(8,128)S(1)} %all_sum_1.1.factor, bf16[2,1024,256]{2,1,0:T(8,128)(2,1)S(1)} %get-tuple-element.21.hn, bf16[2,1024,256]{2,1,0:T(8,128)(2,1)S(1)} %get-tuple-element.22.ln, bf16[3,1024,512]{2,1,0:T(8,128)(2,1)S(1)} %get-tuple-element.23.hs, bf16[3,1024,512]{2,1,0:T(8,128)(2,1)S(1)} %get-tuple-element.24.ls), custom_call_target="tpu_custom_call" | custom-call | tf_op jit(solution)/shard_map/left/pallas_call | solution.py:422
  69.9 20.6 %all_sum_0.3 = f32[1280,128]{1,0:T(8,128)S(1)} custom-call(f32[1280,128]{1,0:T(8,128)S(1)} %bitcast.38), custom_call_target="tpu_custom_call" | custom-call | tf_op jit(solution)/shard_map/all_sum_0/pallas_call | solution.py:344
  90.4 0.0 copy-start.4
  90.5 0.0 copy-start.6
  90.5 8.0 %right.3 = (f32[8,160,128]{2,1,0:T(8,128)S(1)}, f32[512,128]{1,0:T(8,128)S(1)}) custom-call(f32[8,160,128]{2,1,0:T(8,128)S(1)} %bitcast.37, bf16[2,1024,256]{2,1,0:T(8,128)(2,1)S(1)} %get-tuple-element.21.hn, bf16[2,1024,256]{2,1,0:T(8,128)(2,1)S(1)} %get-tuple-element.22.ln, bf16[3,1024,512]{2,1,0:T(8,128)(2,1)S(1)} %get-tuple-element.23.hs, ...), custom_call_target="tpu_custom_call" | custom-call | tf_op jit(solution)/shard_map/right/pallas_call | solution.py:434
  98.4 20.1 %all_sum_2.1.both = f32[1024,128]{1,0:T(8,128)S(1)} custom-call(f32[512,128]{1,0:T(8,128)S(1)} %get-tuple-element.27.x), custom_call_target="tpu_custom_call" | custom-call | tf_op jit(solution)/shard_map/all_sum_2/pallas_call | solution.py:344
  118.5 0.0 copy-done.4
  118.5 0.0 copy-done.6
  118.6 5.4 %last.1 = (f32[2,1024,256]{2,1,0:T(8,128)}, f32[3,1024,512]{2,1,0:T(8,128)}, f32[2,32,256]{2,1,0:T(8,128)}, f32[3,32,512]{2,1,0:T(8,128)}, f32[256,128]{1,0:T(8,128)}, /*index=5*/f32[768,128]{1,0:T(8,128)}) custom-call(f32[8,160,128]{2,1,0:T(8,128)S(1)} %get-tuple-element.26.ortho, f32[1024,128]{1,0:T(8,128)S(1)} %all_sum_2.1.both, ...), custom_call_target="tpu_custom_call" | custom-call | tf_op jit(solution)/shard_map/last/pallas_call | solution.py:446
  (1 shorter events, 0.0 us)
Async XLA Ops:
  0.6 2.8 %copy-start = (f32[1,1,3,1024,512]{4,3,2,1,0:T(8,128)S(1)}, f32[1,1,3,1024,512]{4,3,2,1,0:T(8,128)}, u32[]{:S(2)}) copy-start(f32[1,1,3,1024,512]{4,3,2,1,0:T(8,128)} %param.13) | copy-start | bytes 18874372
  3.4 1.9 %copy-start.1 = (bf16[1,1,3,1024,512]{4,3,2,1,0:T(8,128)(2,1)S(1)}, bf16[1,1,3,1024,512]{4,3,2,1,0:T(8,128)(2,1)}, u32[]{:S(2)}) copy-start(bf16[1,1,3,1024,512]{4,3,2,1,0:T(8,128)(2,1)} %param.12) | copy-start | bytes 9437188
  5.3 1.6 %copy-start.2 = (f32[1,1,2,1024,256]{4,3,2,1,0:T(8,128)S(1)}, f32[1,1,2,1024,256]{4,3,2,1,0:T(8,128)}, u32[]{:S(2)}) copy-start(f32[1,1,2,1024,256]{4,3,2,1,0:T(8,128)} %param.9) | copy-start | bytes 6291460
  6.9 1.2 copy-start.3
  8.1 0.9 copy-start.5
  9.1 0.8 copy-start.7
  90.4 28.1 %copy-start.4 = (f32[1,3,32768]{2,0,1:T(1,128)S(1)}, f32[1,3,32768]{2,0,1:T(1,128)}, u32[]{:S(2)}) copy-start(f32[1,3,32768]{2,0,1:T(1,128)} %param.15) | copy-start | bytes 1179652
  90.5 28.1 %copy-start.6 = (f32[1,2,16384]{2,1,0:T(2,128)S(1)}, f32[1,2,16384]{2,1,0:T(2,128)}, u32[]{:S(2)}) copy-start(f32[1,2,16384]{2,1,0:T(2,128)} %param.11) | copy-start | bytes 393220
